TPU v7x, 32 devices: a whole 2x2x4 slice. The times are simulated.
32 devices in a mesh: groups: 2 (over y), inst: 4 (over z), space: 4 (over x, core).
Axes of the slice: x: 2, y: 2, z: 4, core: 2. Of those that a mesh axis runs over, the one named last changes fastest.
Arguments:
- flow_state: float32 [8, 5, 16, 16, 128], P(('groups', 'inst'), None, 'space'), parts along dimension 0, may hold values from -1 to 1
- period_match: int32 [16], replicated, may hold values from 0 to 15, each once
Outputs:
- residual: float32 [8, 5, 16, 16, 128], P(('groups', 'inst'), None, 'space'), parts along dimension 0
There are 2 independent parts, one for each index of `groups`. A program takes and returns all parts, laid end to end along the dimension named above; an argument that names none is the same for every part. Nothing has to cross between parts.
Inputs may be any that keep to these rules, and one draw needn't show every extreme that they name: period_match is a permutation of the 16 spanwise layers.
All inputs are finite; a program needn't handle non-finite values.
Results may differ from a plain program's by a relative error of at most 0.0003.
Values sent between devices are 32-bit elements; how exact they have to be, the bound alone decides.
No kernel may reach another device: no remote copies, remote signals or barrier semaphores. Data moves between devices by JAX's collectives and lax.ppermute only.
A program may use at most 64 MiB of HBM per device.

v0:
```python
import math
import jax
import jax.numpy as jnp
from jax import lax
from jax.sharding import PartitionSpec as P

gamma_gas = 1.4
prandtl = 0.72
viscosity = 0.1
pseudo_step = 0.03
entropy_share = 0.1


def from_behind(block, axis, distance):
    devices = range(lax.axis_size(axis))
    route = [((i - distance) % len(devices), i) for i in devices]
    return lax.ppermute(block, axis, route)


def extended(cells, sides, width):
    for axis, dim in sides:
        count = lax.axis_size(axis)
        ends = count - 1
        head = lax.slice_in_dim(cells, 0, width, axis=dim)
        tail = lax.slice_in_dim(cells, cells.shape[dim] - width, cells.shape[dim], axis=dim)
        cells = jnp.concatenate(
            [
                lax.ppermute(tail, axis, [(i, (i + 1) % count) for i in range(ends)]),
                cells,
                lax.ppermute(head, axis, [((i + 1) % count, i) for i in range(ends)]),
            ],
            axis=dim,
        )
    return cells


def from_draw(draws):
    shape = (5,) + (1,) * (draws.ndim - 1)
    offsets = jnp.array([1.0, 0.8, 0.0, 0.0, 0.8], jnp.float32).reshape(shape)
    spreads = jnp.array([0.3, 0.3, 0.3, 0.3, 0.2], jnp.float32).reshape(shape)
    return offsets + spreads * draws


def conserved(primitives):
    dens = primitives[0]
    velocity = primitives[1:4]
    kinetic = 0.5 * dens * jnp.sum(velocity * velocity, axis=0)
    energy = primitives[4] / (gamma_gas - 1.0) + kinetic
    return jnp.concatenate([dens[None], dens[None] * velocity, energy[None]], axis=0)


def primitive(conserved_vars):
    dens = conserved_vars[0]
    velocity = conserved_vars[1:4] / dens
    pressure = (gamma_gas - 1.0) * (
        conserved_vars[4] - 0.5 * dens * jnp.sum(velocity * velocity, axis=0)
    )
    return jnp.concatenate([dens[None], velocity, pressure[None]], axis=0)


def entropy_fix(eigen_val, sound_speed):
    spread = entropy_share * sound_speed
    magnitude = jnp.abs(eigen_val)
    return jnp.where(
        magnitude >= spread, magnitude, (eigen_val * eigen_val + spread * spread) / (2.0 * spread)
    )


def euler_flux(dens, velocity, pressure, enthalpy, normal):
    normal_vel = velocity[normal]
    values = [dens * normal_vel]
    for component in range(3):
        moment = dens * velocity[component] * normal_vel
        if component == normal:
            moment = moment + pressure
        values.append(moment)
    values.append(dens * enthalpy * normal_vel)
    return values


def face_flux(left_cells, right_cells, normal):
    dens_left, vel_left, pres_left = (left_cells[0], left_cells[1:4], left_cells[4])
    dens_right, vel_right, pres_right = (right_cells[0], right_cells[1:4], right_cells[4])
    ratio = gamma_gas / (gamma_gas - 1.0)
    sq_left = jnp.sum(vel_left * vel_left, axis=0)
    sq_right = jnp.sum(vel_right * vel_right, axis=0)
    enth_left = ratio * pres_left / dens_left + 0.5 * sq_left
    enth_right = ratio * pres_right / dens_right + 0.5 * sq_right
    flux_left = euler_flux(dens_left, vel_left, pres_left, enth_left, normal)
    flux_right = euler_flux(dens_right, vel_right, pres_right, enth_right, normal)
    root_left = jnp.sqrt(dens_left)
    root_right = jnp.sqrt(dens_right)
    root_sum = root_left + root_right
    vel_roe = (root_left * vel_left + root_right * vel_right) / root_sum
    enth_roe = (root_left * enth_left + root_right * enth_right) / root_sum
    speed_sq = jnp.sum(vel_roe * vel_roe, axis=0)
    sound_sq = (gamma_gas - 1.0) * (enth_roe - 0.5 * speed_sq)
    sound_speed = jnp.sqrt(sound_sq)
    normal_vel = vel_roe[normal]
    dens_roe = root_left * root_right
    jump_dens = dens_right - dens_left
    jump_pres = pres_right - pres_left
    jump_vel = vel_right - vel_left
    jump_normal = jump_vel[normal]
    wave_slow = (jump_pres - dens_roe * sound_speed * jump_normal) / (2.0 * sound_sq)
    wave_fast = (jump_pres + dens_roe * sound_speed * jump_normal) / (2.0 * sound_sq)
    wave_mid = jump_dens - jump_pres / sound_sq
    eigen_mid = entropy_fix(normal_vel, sound_speed)
    flux_slow = entropy_fix(normal_vel - sound_speed, sound_speed) * wave_slow
    flux_fast = entropy_fix(normal_vel + sound_speed, sound_speed) * wave_fast
    dissipation = [flux_slow + eigen_mid * wave_mid + flux_fast]
    for component in range(3):
        unit_dir = 1.0 if component == normal else 0.0
        term = flux_slow * (vel_roe[component] - unit_dir * sound_speed)
        term = term + eigen_mid * (
            wave_mid * vel_roe[component]
            + dens_roe * (jump_vel[component] - unit_dir * jump_normal)
        )
        term = term + flux_fast * (vel_roe[component] + unit_dir * sound_speed)
        dissipation.append(term)
    shear_work = jnp.sum(vel_roe * jump_vel, axis=0) - normal_vel * jump_normal
    energy_term = flux_slow * (enth_roe - normal_vel * sound_speed)
    energy_term = energy_term + eigen_mid * (wave_mid * 0.5 * speed_sq + dens_roe * shear_work)
    energy_term = energy_term + flux_fast * (enth_roe + normal_vel * sound_speed)
    dissipation.append(energy_term)
    jump_temp = pres_right / dens_right - pres_left / dens_left
    jump_kin = 0.5 * (sq_right - sq_left)
    viscous_terms = [
        jnp.zeros_like(jump_dens),
        jump_vel[0],
        jump_vel[1],
        jump_vel[2],
        jump_kin + gamma_gas / ((gamma_gas - 1.0) * prandtl) * jump_temp,
    ]
    values = []
    for component in range(5):
        values.append(
            0.5 * (flux_left[component] + flux_right[component])
            - 0.5 * dissipation[component]
            - viscosity * viscous_terms[component]
        )
    return jnp.stack(values, axis=0)


def flux_change(padded, along, normal):
    length = padded.shape[along]
    face_values = face_flux(
        lax.slice_in_dim(padded, 0, length - 1, axis=along),
        lax.slice_in_dim(padded, 1, length, axis=along),
        normal,
    )
    return lax.slice_in_dim(face_values, 1, length - 1, axis=along) - lax.slice_in_dim(
        face_values, 0, length - 2, axis=along
    )


def spectral_entry(offset, number):
    wrapped = jnp.mod(offset, number)
    parity = 1.0 - 2.0 * jnp.mod(wrapped, 2).astype(jnp.float32)
    angles = math.pi * wrapped.astype(jnp.float32) / number
    sine_val = jnp.where(wrapped == 0, 1.0, jnp.sin(angles))
    derivative = jnp.where(
        wrapped == 0, 0.0, math.pi / number * parity * jnp.cos(angles) / sine_val
    )
    return derivative + 0.5 * parity


def on_device(flow_state, period_match):
    instances = lax.axis_size("inst")
    phase_lag = instances // 4
    instance = lax.axis_index("inst")
    space_parts = lax.axis_size("space")
    position = lax.axis_index("space")
    labels = jnp.arange(period_match.shape[0], dtype=jnp.int32)
    matches = (period_match[:, None] == labels[None, :]).astype(jnp.int32)
    inverse = jnp.sum(labels[:, None] * matches, axis=0)
    mirror = jnp.array([1.0, 1.0, 1.0, -1.0, 1.0], jnp.float32).reshape(5, 1, 1, 1)

    def lagged(plane, steps):
        return from_behind(plane, "inst", steps)

    def timewise(conserved_vars):
        pieces = lax.all_gather(conserved_vars[None], "inst", axis=0, tiled=True)
        number = pieces.shape[0]
        others = jnp.arange(number, dtype=jnp.int32)
        weights = spectral_entry(instance - others, instances)
        return jnp.tensordot(weights, pieces, axes=1, precision=lax.Precision.HIGHEST)

    def evaluate(conserved_vars):
        prims = primitive(conserved_vars)
        padded = extended(prims, (("space", 1),), 1)
        lower_edge = jnp.where(position == 0, prims[:, :1], padded[:, :1])
        upper_edge = jnp.where(position == space_parts - 1, prims[:, -1:], padded[:, -1:])
        along_axial = jnp.concatenate([lower_edge, prims, upper_edge], axis=1)
        along_span = jnp.concatenate(
            [prims[:, :, :1] * mirror, prims, prims[:, :, -1:] * mirror], axis=2
        )
        ghost_below = jnp.take(lagged(prims[..., -1], phase_lag), period_match, axis=2)
        ghost_above = jnp.take(lagged(prims[..., 0], -phase_lag), inverse, axis=2)
        along_pitch = jnp.concatenate(
            [ghost_below[..., None], prims, ghost_above[..., None]], axis=3
        )
        spatial = (
            flux_change(along_axial, 1, 0)
            + flux_change(along_span, 2, 2)
            + flux_change(along_pitch, 3, 1)
        )
        return timewise(conserved_vars) + spatial

    initial = conserved(from_draw(flow_state[0]))
    section_state = initial - pseudo_step * evaluate(initial)
    return evaluate(section_state)[None]


def solution(mesh):
    in_specs = (P(("groups", "inst"), None, "space", None, None), P())
    out_specs = P(("groups", "inst"), None, "space", None, None)
    return jax.shard_map(
        on_device, mesh=mesh, in_specs=in_specs, out_specs=out_specs, check_vma=False
    )
```

profile of v0, /device:TPU:1, one launch (start us, length us, event | category | flops | bytes accessed | tf_op | source)
XLA Modules:
  0.0 72.5 jit_solution(7410314620236597218)
XLA Ops:
  0.0 0.7 copy-done.1
  0.7 1.0 %fusion.15 = f32[5,4,16,128]{3,2,1,0:T(8,128)S(1)} fusion(f32[1,5,4,16,128]{4,3,2,1,0:T(8,128)} %param.7, f32[5]{0:T(128)S(1)} %copy-done.1, f32[5]{0:T(128)S(1)} %copy-done.2), kind=kLoop, calls=%fused_computation.59 | loop fusion | flops 81920 | bytes 327720 | tf_op jit(solution)/shard_map/add | solution.py:41
  1.9 0.5 copy.46
  2.4 2.2 %collective-permute-start.2 = (f32[5,4,16]{0,1,2:T(4,128)S(1)}, f32[5,4,16]{0,1,2:T(4,128)S(1)}, u32[]{:S(2)}, u32[]{:S(2)}) collective-permute-start(f32[5,4,16]{0,1,2:T(4,128)S(1)} %bitcast.389), channel_id=1, source_target_pairs={{12,0},{0,4},{4,8},{8,12},{13,1},{1,5},{5,9},{9,13},{14,2},{2,6},{... | collective-permute-start | bytes 3848 | tf_op jit(solution)/shard_map/ppermute | solution.py:17
  5.0 2.1 %collective-permute-start.3 = (f32[5,4,16]{0,1,2:T(4,128)S(1)}, f32[5,4,16]{0,1,2:T(4,128)S(1)}, u32[]{:S(2)}, u32[]{:S(2)}) collective-permute-start(f32[5,4,16]{0,1,2:T(4,128)S(1)} %bitcast.388), channel_id=1, source_target_pairs={{4,0},{8,4},{12,8},{0,12},{5,1},{9,5},{13,9},{1,13},{6,2},{10,6},{... | collective-permute-start | bytes 3848 | tf_op jit(solution)/shard_map/ppermute | solution.py:17
  7.1 4.2 %collective-permute-start = (f32[5,1,16,128]{3,2,1,0:T(8,128)S(1)}, f32[5,1,16,128]{3,2,1,0:T(8,128)S(1)}, u32[]{:S(2)}, u32[]{:S(2)}) collective-permute-start(f32[5,1,16,128]{3,2,1,0:T(8,128)S(1)} %get-tuple-element.119), channel_id=1, source_target_pairs={{0,1},{1,2},{2,3},{4,5},{5,6},{6,7},{8,9},{9,10},{10,11},{12,13},{... | collective-permute-start | bytes 122888 | tf_op jit(solution)/shard_map/ppermute | solution.py:28
  11.3 1.9 %collective-permute-start.1 = (f32[5,1,16,128]{3,2,1,0:T(8,128)S(1)}, f32[5,1,16,128]{3,2,1,0:T(8,128)S(1)}, u32[]{:S(2)}, u32[]{:S(2)}) collective-permute-start(f32[5,1,16,128]{3,2,1,0:T(8,128)S(1)} %get-tuple-element.120), channel_id=1, source_target_pairs={{1,0},{2,1},{3,2},{5,4},{6,5},{7,6},{9,8},{10,9},{11,10},{13,12},{... | collective-permute-start | bytes 122888 | tf_op jit(solution)/shard_map/ppermute | solution.py:30
  13.4 13.8 %all-gather = f32[20,4,16,128]{3,2,1,0:T(8,128)S(1)} all-gather(f32[5,4,16,128]{3,2,1,0:T(8,128)S(1)} %get-tuple-element.130), channel_id=2, replica_groups=mesh['groups'=2,'inst'=4,'space'=4] {'inst'}, dimensions={0}, use_global_device_ids=true | all-gather | bytes 819200 | tf_op jit(solution)/shard_map/all_gather | solution.py:183
  27.2 0.6 copy-done
  28.6 1.5 %fusion.2 = f32[1,5,4,16,128]{4,0,3,2,1:T(1,128)S(1)} fusion(f32[4,5,4,16,128]{4,3,2,1,0:T(8,128)S(1)} %bitcast.384, s32[]{:T(128)S(6)} %axis_index.23), kind=kOutput, calls=%fused_computation.6 | convolution fusion | flops 1966224 | bytes 819204 | tf_op jit(solution)/shard_map/dot_general | solution.py:187
  30.3 0.6 gather_fusion
  31.0 0.6 copy.31
  31.6 0.6 gather_fusion.1
  32.3 0.6 copy.34
  34.9 14.5 %all-gather.1 = f32[20,4,16,128]{3,2,1,0:T(8,128)S(1)} all-gather(f32[5,4,16,128]{3,2,1,0:T(8,128)S(1)} %fusion.13), channel_id=3, replica_groups=mesh['groups'=2,'inst'=4,'space'=4] {'inst'}, dimensions={0}, use_global_device_ids=true | all-gather | bytes 819200 | tf_op jit(solution)/shard_map/all_gather | solution.py:183
  49.6 1.5 %fusion = f32[1,5,4,16,128]{4,0,3,2,1:T(1,128)S(1)} fusion(f32[4,5,4,16,128]{4,3,2,1,0:T(8,128)S(1)} %bitcast.385, s32[]{:T(128)S(6)} %axis_index.23), kind=kOutput, calls=%fused_computation.4 | convolution fusion | flops 1966224 | bytes 819204 | tf_op jit(solution)/shard_map/dot_general | solution.py:187
  52.2 3.3 %collective-permute-start.7 = (f32[5,4,16]{0,1,2:T(4,128)S(1)}, f32[5,4,16]{0,1,2:T(4,128)S(1)}, u32[]{:S(2)}, u32[]{:S(2)}) collective-permute-start(f32[5,4,16]{0,1,2:T(4,128)S(1)} %bitcast.390), channel_id=1, source_target_pairs={{4,0},{8,4},{12,8},{0,12},{5,1},{9,5},{13,9},{1,13},{6,2},{10,6},{... | collective-permute-start | bytes 3848 | tf_op jit(solution)/shard_map/ppermute | solution.py:17
  56.1 8.9 %collective-permute-start.4 = (f32[5,1,16,128]{3,2,1,0:T(8,128)S(1)}, f32[5,1,16,128]{3,2,1,0:T(8,128)S(1)}, u32[]{:S(2)}, u32[]{:S(2)}) collective-permute-start(f32[5,1,16,128]{3,2,1,0:T(8,128)S(1)} %get-tuple-element.105), channel_id=1, source_target_pairs={{0,1},{1,2},{2,3},{4,5},{5,6},{6,7},{8,9},{9,10},{10,11},{12,13},{... | collective-permute-start | bytes 122888 | tf_op jit(solution)/shard_map/ppermute | solution.py:28
  65.0 2.1 %collective-permute-start.5 = (f32[5,1,16,128]{3,2,1,0:T(8,128)S(1)}, f32[5,1,16,128]{3,2,1,0:T(8,128)S(1)}, u32[]{:S(2)}, u32[]{:S(2)}) collective-permute-start(f32[5,1,16,128]{3,2,1,0:T(8,128)S(1)} %get-tuple-element.106), channel_id=1, source_target_pairs={{1,0},{2,1},{3,2},{5,4},{6,5},{7,6},{9,8},{10,9},{11,10},{13,12},{... | collective-permute-start | bytes 122888 | tf_op jit(solution)/shard_map/ppermute | solution.py:30
  67.3 0.6 gather_fusion.2
  68.0 0.6 copy.36
  68.5 0.6 gather_fusion.3
  69.2 0.6 copy.39
  71.7 0.8 %fusion.8 = f32[1,5,4,16,128]{4,3,2,1,0:T(8,128)} fusion(f32[5,4,16,128]{3,2,1,0:T(8,128)S(1)} %bitcast.386, f32[5,4,16,129]{3,2,1,0:T(8,128)S(1)} %fusion.50, f32[5,4,17,128]{3,2,1,0:T(8,128)S(1)} %constant_dynamic-update-slice_fusion.15, f32[5,5,16,128]{3,2,1,0:T(8,128)S(1)} %constant_dynamic-update-slice_fusion.10), kind=kLoop, calls=%fused_computation.45 | loop fusion | flops 245760 | bytes 1310720 | tf_op jit(solution)/shard_map/broadcast_in_dim | solution.py:212
  (94 shorter events, 7.8 us)
Async XLA Ops:
  0.0 0.7 copy-start.1
  0.0 0.7 copy-start.2
  2.4 27.9 %collective-permute-start.2 = (f32[5,4,16]{0,1,2:T(4,128)S(1)}, f32[5,4,16]{0,1,2:T(4,128)S(1)}, u32[]{:S(2)}, u32[]{:S(2)}) collective-permute-start(f32[5,4,16]{0,1,2:T(4,128)S(1)} %bitcast.389), channel_id=1, source_target_pairs={{12,0},{0,4},{4,8},{8,12},{13,1},{1,5},{5,9},{9,13},{14,2},{2,6},{... | collective-permute-start | bytes 3848 | tf_op jit(solution)/shard_map/ppermute | solution.py:17
  5.0 26.5 %collective-permute-start.3 = (f32[5,4,16]{0,1,2:T(4,128)S(1)}, f32[5,4,16]{0,1,2:T(4,128)S(1)}, u32[]{:S(2)}, u32[]{:S(2)}) collective-permute-start(f32[5,4,16]{0,1,2:T(4,128)S(1)} %bitcast.388), channel_id=1, source_target_pairs={{4,0},{8,4},{12,8},{0,12},{5,1},{9,5},{13,9},{1,13},{6,2},{10,6},{... | collective-permute-start | bytes 3848 | tf_op jit(solution)/shard_map/ppermute | solution.py:17
  7.1 26.9 %collective-permute-start = (f32[5,1,16,128]{3,2,1,0:T(8,128)S(1)}, f32[5,1,16,128]{3,2,1,0:T(8,128)S(1)}, u32[]{:S(2)}, u32[]{:S(2)}) collective-permute-start(f32[5,1,16,128]{3,2,1,0:T(8,128)S(1)} %get-tuple-element.119), channel_id=1, source_target_pairs={{0,1},{1,2},{2,3},{4,5},{5,6},{6,7},{8,9},{9,10},{10,11},{12,13},{... | collective-permute-start | bytes 122888 | tf_op jit(solution)/shard_map/ppermute | solution.py:28
  11.3 1.9 %copy-start.3 = (s32[16]{0:T(128)S(1)}, s32[16]{0:T(128)}, u32[]{:S(2)}) copy-start(s32[16]{0:T(128)} %param.8) | copy-start | bytes 196
  11.3 22.7 %collective-permute-start.1 = (f32[5,1,16,128]{3,2,1,0:T(8,128)S(1)}, f32[5,1,16,128]{3,2,1,0:T(8,128)S(1)}, u32[]{:S(2)}, u32[]{:S(2)}) collective-permute-start(f32[5,1,16,128]{3,2,1,0:T(8,128)S(1)} %get-tuple-element.120), channel_id=1, source_target_pairs={{1,0},{2,1},{3,2},{5,4},{6,5},{7,6},{9,8},{10,9},{11,10},{13,12},{... | collective-permute-start | bytes 122888 | tf_op jit(solution)/shard_map/ppermute | solution.py:30
  27.2 0.7 copy-start
  51.7 15.6 %collective-permute-start.6 = (f32[5,4,16]{0,1,2:T(4,128)S(1)}, f32[5,4,16]{0,1,2:T(4,128)S(1)}, u32[]{:S(2)}, u32[]{:S(2)}) collective-permute-start(f32[5,4,16]{0,1,2:T(4,128)S(1)} %bitcast.391), channel_id=1, source_target_pairs={{12,0},{0,4},{4,8},{8,12},{13,1},{1,5},{5,9},{9,13},{14,2},{2,6},{... | collective-permute-start | bytes 3848 | tf_op jit(solution)/shard_map/ppermute | solution.py:17
  52.2 16.3 %collective-permute-start.7 = (f32[5,4,16]{0,1,2:T(4,128)S(1)}, f32[5,4,16]{0,1,2:T(4,128)S(1)}, u32[]{:S(2)}, u32[]{:S(2)}) collective-permute-start(f32[5,4,16]{0,1,2:T(4,128)S(1)} %bitcast.390), channel_id=1, source_target_pairs={{4,0},{8,4},{12,8},{0,12},{5,1},{9,5},{13,9},{1,13},{6,2},{10,6},{... | collective-permute-start | bytes 3848 | tf_op jit(solution)/shard_map/ppermute | solution.py:17
  56.1 14.8 %collective-permute-start.4 = (f32[5,1,16,128]{3,2,1,0:T(8,128)S(1)}, f32[5,1,16,128]{3,2,1,0:T(8,128)S(1)}, u32[]{:S(2)}, u32[]{:S(2)}) collective-permute-start(f32[5,1,16,128]{3,2,1,0:T(8,128)S(1)} %get-tuple-element.105), channel_id=1, source_target_pairs={{0,1},{1,2},{2,3},{4,5},{5,6},{6,7},{8,9},{9,10},{10,11},{12,13},{... | collective-permute-start | bytes 122888 | tf_op jit(solution)/shard_map/ppermute | solution.py:28
  65.0 5.9 %collective-permute-start.5 = (f32[5,1,16,128]{3,2,1,0:T(8,128)S(1)}, f32[5,1,16,128]{3,2,1,0:T(8,128)S(1)}, u32[]{:S(2)}, u32[]{:S(2)}) collective-permute-start(f32[5,1,16,128]{3,2,1,0:T(8,128)S(1)} %get-tuple-element.106), channel_id=1, source_target_pairs={{1,0},{2,1},{3,2},{5,4},{6,5},{7,6},{9,8},{10,9},{11,10},{13,12},{... | collective-permute-start | bytes 122888 | tf_op jit(solution)/shard_map/ppermute | solution.py:30
where the time goes:
time: 72.7 us; the launch traced here: 72.5 us
  blocking collectives  28.3 us (39%)
  starting transfers between devices  24.6 us (34%)
  local copies, waits for them, and re-layouts  8.14 us (11%)
  other arithmetic  7.8 us (11%)
  matrix products  3.1 us (4%)
    all_gather x2, blocking collectives, timewise(): pieces = lax.all_gather(conserved_vars[None], 'inst', axis=0, tiled=True)  28.3 us
    ppermute x2, starting transfers between devices, extended(): lax.ppermute(tail, axis, [(i, (i + 1) % count) for i in range(ends)])  13 us
    ppermute x4, starting transfers between devices, from_behind(): return lax.ppermute(block, axis, route)  7.53 us
    ppermute x2, starting transfers between devices, extended(): lax.ppermute(head, axis, [((i + 1) % count, i) for i in range(ends)])  4.02 us
    dot_general x2, matrix products, timewise(): jnp.tensordot(weights, pieces, axes=1, precision=lax.Precision.HIGHEST)  3.1 us
    unnamed x24, other arithmetic  3.02 us
  transfers between devices with their start and end apart: 8, of which 0 were waited for; matrix products, arithmetic and copies ran while one was open for 16% of the time, Pallas kernels for 0%

commit v1 on v0

--- a/solution.py
+++ b/solution.py
@@ -180,7 +180,14 @@
         return from_behind(plane, "inst", steps)
 
     def timewise(conserved_vars):
-        pieces = lax.all_gather(conserved_vars[None], "inst", axis=0, tiled=True)
+        ring = [conserved_vars[None]]
+        for hop in range(3):
+            ring.append(lax.ppermute(ring[-1], "inst", [(dev, (dev + 1) % 4) for dev in range(4)]))
+        pieces = jnp.roll(
+            jnp.concatenate(ring[::-1], axis=0),
+            (lax.axis_index("inst") + 1) * ring[0].shape[0],
+            axis=0,
+        )
         number = pieces.shape[0]
         others = jnp.arange(number, dtype=jnp.int32)
         weights = spectral_entry(instance - others, instances)

time: 72.7 us -> 68 us (0.935)
  blocking collectives: 28.3 us -> 0 us
  waiting for transfers between devices: 0.02 us -> 25.1 us
  starting transfers between devices: 24.6 us -> 22.8 us
  local copies, waits for them, and re-layouts: 8.14 us -> 6.83 us
  other arithmetic: 7.8 us -> 8.55 us
    all_gather x2 -> x0, blocking collectives: 28.3 us -> none  [timewise(): pieces = lax.all_gather(conserved_vars[None], 'inst', axis=0, tiled=True)]
    ppermute x0 -> x6, waiting for transfers between devices: none -> 25.1 us  [timewise(): lax.ppermute(ring[-1], 'inst', [(dev, (dev + 1) % 4) for dev in range(4)])]
    ppermute x2, starting transfers between devices: 13 us -> 9.98 us  [extended(): lax.ppermute(tail, axis, [(i, (i + 1) % count) for i in range(ends)])]
    ppermute x0 -> x6, starting transfers between devices: none -> 2.36 us  [timewise(): lax.ppermute(ring[-1], 'inst', [(dev, (dev + 1) % 4) for dev in range(4)])]
    unnamed x8 -> x4, local copies, waits for them, and re-layouts: 1.32 us -> 0.01 us
    ppermute x4, starting transfers between devices: 7.53 us -> 6.62 us  [from_behind(): return lax.ppermute(block, axis, route)]
    concatenate x0 -> x2, other arithmetic: none -> 0.75 us  [timewise(): jnp.roll(jnp.concatenate(ring[::-1], axis=0), (lax.axis_index('inst') + 1...]
  transfers between devices with their start and end apart: 8 -> 14, of which waited for: 0 -> 4; matrix products, arithmetic and copies ran while one was open for 16% -> 18% of each run, Pallas kernels for 0% -> 0%
where the time goes in v1:
time: 68 us; the launch traced here: 67.1 us
  waiting for transfers between devices  25.1 us (37%)
  starting transfers between devices  22.8 us (34%)
  other arithmetic  8.55 us (13%)
  local copies, waits for them, and re-layouts  6.83 us (10%)
  matrix products  3.1 us (5%)
    ppermute x6, waiting for transfers between devices, timewise(): lax.ppermute(ring[-1], 'inst', [(dev, (dev + 1) % 4) for dev in range(4)])  25.1 us
    ppermute x2, starting transfers between devices, extended(): lax.ppermute(tail, axis, [(i, (i + 1) % count) for i in range(ends)])  9.98 us
    ppermute x4, starting transfers between devices, from_behind(): return lax.ppermute(block, axis, route)  6.62 us
    ppermute x2, starting transfers between devices, extended(): lax.ppermute(head, axis, [((i + 1) % count, i) for i in range(ends)])  3.84 us
    dot_general x2, matrix products, timewise(): jnp.tensordot(weights, pieces, axes=1, precision=lax.Precision.HIGHEST)  3.1 us
    unnamed x24, other arithmetic  3.01 us
    ppermute x6, starting transfers between devices, timewise(): lax.ppermute(ring[-1], 'inst', [(dev, (dev + 1) % 4) for dev in range(4)])  2.36 us
  transfers between devices with their start and end apart: 14, of which 4 were waited for; matrix products, arithmetic and copies ran while one was open for 18% of the time, Pallas kernels for 0%

profile of v1, /device:TPU:1, one launch (start us, length us, event | category | flops | bytes accessed | tf_op | source)
XLA Modules:
  0.0 67.1 jit_solution(5233077839174097120)
XLA Ops:
  0.0 1.0 %fusion.29 = f32[5,4,16,128]{3,2,1,0:T(8,128)S(1)} fusion(f32[1,5,4,16,128]{4,3,2,1,0:T(8,128)} %param.9, f32[5]{0:T(128)} %constant.139.clone, f32[5]{0:T(128)} %constant.138.clone), kind=kLoop, calls=%fused_computation.89 | loop fusion | flops 81920 | bytes 327720 | tf_op jit(solution)/shard_map/add | solution.py:41
  1.2 2.2 %collective-permute-start = (f32[1,5,4,16,128]{4,3,2,1,0:T(8,128)S(1)}, f32[1,5,4,16,128]{4,3,2,1,0:T(8,128)S(1)}, u32[]{:S(2)}, u32[]{:S(2)}) collective-permute-start(f32[1,5,4,16,128]{4,3,2,1,0:T(8,128)S(1)} %get-tuple-element.132), channel_id=1, source_target_pairs={{0,4},{4,8},{8,12},{12,0},{1,5},{5,9},{9,13},{13,1},{2,6},{6,10},{... | collective-permute-start | bytes 491528 | tf_op jit(solution)/shard_map/ppermute | solution.py:185
  3.9 1.3 %collective-permute-start.5 = (f32[5,4,16]{0,1,2:T(4,128)S(1)}, f32[5,4,16]{0,1,2:T(4,128)S(1)}, u32[]{:S(2)}, u32[]{:S(2)}) collective-permute-start(f32[5,4,16]{0,1,2:T(4,128)S(1)} %bitcast.390), channel_id=1, source_target_pairs={{12,0},{0,4},{4,8},{8,12},{13,1},{1,5},{5,9},{9,13},{14,2},{2,6},{... | collective-permute-start | bytes 3848 | tf_op jit(solution)/shard_map/ppermute | solution.py:17
  5.8 2.0 %collective-permute-start.6 = (f32[5,4,16]{0,1,2:T(4,128)S(1)}, f32[5,4,16]{0,1,2:T(4,128)S(1)}, u32[]{:S(2)}, u32[]{:S(2)}) collective-permute-start(f32[5,4,16]{0,1,2:T(4,128)S(1)} %bitcast.389), channel_id=1, source_target_pairs={{4,0},{8,4},{12,8},{0,12},{5,1},{9,5},{13,9},{1,13},{6,2},{10,6},{... | collective-permute-start | bytes 3848 | tf_op jit(solution)/shard_map/ppermute | solution.py:17
  7.8 4.5 %collective-permute-start.3 = (f32[5,1,16,128]{3,2,1,0:T(8,128)S(1)}, f32[5,1,16,128]{3,2,1,0:T(8,128)S(1)}, u32[]{:S(2)}, u32[]{:S(2)}) collective-permute-start(f32[5,1,16,128]{3,2,1,0:T(8,128)S(1)} %get-tuple-element.120), channel_id=1, source_target_pairs={{0,1},{1,2},{2,3},{4,5},{5,6},{6,7},{8,9},{9,10},{10,11},{12,13},{... | collective-permute-start | bytes 122888 | tf_op jit(solution)/shard_map/ppermute | solution.py:28
  12.3 1.9 %collective-permute-start.4 = (f32[5,1,16,128]{3,2,1,0:T(8,128)S(1)}, f32[5,1,16,128]{3,2,1,0:T(8,128)S(1)}, u32[]{:S(2)}, u32[]{:S(2)}) collective-permute-start(f32[5,1,16,128]{3,2,1,0:T(8,128)S(1)} %get-tuple-element.121), channel_id=1, source_target_pairs={{1,0},{2,1},{3,2},{5,4},{6,5},{7,6},{9,8},{10,9},{11,10},{13,12},{... | collective-permute-start | bytes 122888 | tf_op jit(solution)/shard_map/ppermute | solution.py:30
  15.3 0.6 gather_fusion
  16.0 0.6 copy.20
  16.6 0.6 gather_fusion.1
  17.2 0.6 copy.23
  19.7 5.9 %collective-permute-done.1 = f32[1,5,4,16,128]{4,3,2,1,0:T(8,128)S(1)} collective-permute-done((f32[1,5,4,16,128]{4,3,2,1,0:T(8,128)S(1)}, f32[1,5,4,16,128]{4,3,2,1,0:T(8,128)S(1)}, u32[]{:S(2)}, u32[]{:S(2)}) %collective-permute-start.1) | collective-permute-done | bytes 163872 | tf_op jit(solution)/shard_map/ppermute | solution.py:185
  25.6 6.9 %collective-permute-done.2 = f32[1,5,4,16,128]{4,3,2,1,0:T(8,128)S(1)} collective-permute-done((f32[1,5,4,16,128]{4,3,2,1,0:T(8,128)S(1)}, f32[1,5,4,16,128]{4,3,2,1,0:T(8,128)S(1)}, u32[]{:S(2)}, u32[]{:S(2)}) %collective-permute-start.2) | collective-permute-done | bytes 163872 | tf_op jit(solution)/shard_map/ppermute | solution.py:185
  32.9 1.5 %fusion.16 = f32[1,5,4,16,128]{4,0,3,2,1:T(1,128)S(1)} fusion(f32[4,5,4,16,128]{4,3,2,1,0:T(8,128)S(1)} %fusion.10, s32[]{:T(128)S(6)} %axis_index.15), kind=kOutput, calls=%fused_computation.36 | convolution fusion | flops 1966224 | bytes 819204 | tf_op jit(solution)/shard_map/dot_general | solution.py:194
  36.0 3.3 %collective-permute-start.13 = (f32[5,4,16]{0,1,2:T(4,128)S(1)}, f32[5,4,16]{0,1,2:T(4,128)S(1)}, u32[]{:S(2)}, u32[]{:S(2)}) collective-permute-start(f32[5,4,16]{0,1,2:T(4,128)S(1)} %bitcast.391), channel_id=1, source_target_pairs={{4,0},{8,4},{12,8},{0,12},{5,1},{9,5},{13,9},{1,13},{6,2},{10,6},{... | collective-permute-start | bytes 3848 | tf_op jit(solution)/shard_map/ppermute | solution.py:17
  39.9 5.5 %collective-permute-start.10 = (f32[5,1,16,128]{3,2,1,0:T(8,128)S(1)}, f32[5,1,16,128]{3,2,1,0:T(8,128)S(1)}, u32[]{:S(2)}, u32[]{:S(2)}) collective-permute-start(f32[5,1,16,128]{3,2,1,0:T(8,128)S(1)} %get-tuple-element.106), channel_id=1, source_target_pairs={{0,1},{1,2},{2,3},{4,5},{5,6},{6,7},{8,9},{9,10},{10,11},{12,13},{... | collective-permute-start | bytes 122888 | tf_op jit(solution)/shard_map/ppermute | solution.py:28
  45.4 1.9 %collective-permute-start.11 = (f32[5,1,16,128]{3,2,1,0:T(8,128)S(1)}, f32[5,1,16,128]{3,2,1,0:T(8,128)S(1)}, u32[]{:S(2)}, u32[]{:S(2)}) collective-permute-start(f32[5,1,16,128]{3,2,1,0:T(8,128)S(1)} %get-tuple-element.107), channel_id=1, source_target_pairs={{1,0},{2,1},{3,2},{5,4},{6,5},{7,6},{9,8},{10,9},{11,10},{13,12},{... | collective-permute-start | bytes 122888 | tf_op jit(solution)/shard_map/ppermute | solution.py:30
  47.5 0.6 gather_fusion.2
  48.1 0.6 copy.25
  48.7 0.6 gather_fusion.3
  49.4 0.6 copy.28
  51.8 5.9 %collective-permute-done.8 = f32[1,5,4,16,128]{4,3,2,1,0:T(8,128)S(1)} collective-permute-done((f32[1,5,4,16,128]{4,3,2,1,0:T(8,128)S(1)}, f32[1,5,4,16,128]{4,3,2,1,0:T(8,128)S(1)}, u32[]{:S(2)}, u32[]{:S(2)}) %collective-permute-start.8) | collective-permute-done | bytes 163872 | tf_op jit(solution)/shard_map/ppermute | solution.py:185
  57.8 6.5 %collective-permute-done.9 = f32[1,5,4,16,128]{4,3,2,1,0:T(8,128)S(1)} collective-permute-done((f32[1,5,4,16,128]{4,3,2,1,0:T(8,128)S(1)}, f32[1,5,4,16,128]{4,3,2,1,0:T(8,128)S(1)}, u32[]{:S(2)}, u32[]{:S(2)}) %collective-permute-start.9) | collective-permute-done | bytes 163872 | tf_op jit(solution)/shard_map/ppermute | solution.py:185
  64.7 1.5 %fusion.14 = f32[1,5,4,16,128]{4,0,3,2,1:T(1,128)S(1)} fusion(f32[4,5,4,16,128]{4,3,2,1,0:T(8,128)S(1)} %fusion.3, s32[]{:T(128)S(6)} %axis_index.15), kind=kOutput, calls=%fused_computation.34 | convolution fusion | flops 1966224 | bytes 819204 | tf_op jit(solution)/shard_map/dot_general | solution.py:194
  66.3 0.8 %fusion.22 = f32[1,5,4,16,128]{4,3,2,1,0:T(8,128)} fusion(f32[5,4,16,128]{3,2,1,0:T(8,128)S(1)} %bitcast.387, f32[5,4,16,129]{3,2,1,0:T(8,128)S(1)} %fusion.65, f32[5,4,17,128]{3,2,1,0:T(8,128)S(1)} %constant_dynamic-update-slice_fusion.15, f32[5,5,16,128]{3,2,1,0:T(8,128)S(1)} %constant_dynamic-update-slice_fusion.10), kind=kLoop, calls=%fused_computation.75 | loop fusion | flops 245760 | bytes 1310720 | tf_op jit(solution)/shard_map/broadcast_in_dim | solution.py:219
  (102 shorter events, 9.2 us)
Async XLA Ops:
  1.1 13.1 %copy-start.1 = (s32[16]{0:T(128)S(1)}, s32[16]{0:T(128)}, u32[]{:S(2)}) copy-start(s32[16]{0:T(128)} %param.10) | copy-start | bytes 196
  1.1 13.2 %copy-start = (f32[5]{0:T(128)S(1)}, f32[5]{0:T(128)}, u32[]{:S(2)}) copy-start(f32[5]{0:T(128)} %constant.137.clone) | copy-start | bytes 64
  1.2 18.3 %collective-permute-start = (f32[1,5,4,16,128]{4,3,2,1,0:T(8,128)S(1)}, f32[1,5,4,16,128]{4,3,2,1,0:T(8,128)S(1)}, u32[]{:S(2)}, u32[]{:S(2)}) collective-permute-start(f32[1,5,4,16,128]{4,3,2,1,0:T(8,128)S(1)} %get-tuple-element.132), channel_id=1, source_target_pairs={{0,4},{4,8},{8,12},{12,0},{1,5},{5,9},{9,13},{13,1},{2,6},{6,10},{... | collective-permute-start | bytes 491528 | tf_op jit(solution)/shard_map/ppermute | solution.py:185
  3.9 11.4 %collective-permute-start.5 = (f32[5,4,16]{0,1,2:T(4,128)S(1)}, f32[5,4,16]{0,1,2:T(4,128)S(1)}, u32[]{:S(2)}, u32[]{:S(2)}) collective-permute-start(f32[5,4,16]{0,1,2:T(4,128)S(1)} %bitcast.390), channel_id=1, source_target_pairs={{12,0},{0,4},{4,8},{8,12},{13,1},{1,5},{5,9},{9,13},{14,2},{2,6},{... | collective-permute-start | bytes 3848 | tf_op jit(solution)/shard_map/ppermute | solution.py:17
  5.8 10.8 %collective-permute-start.6 = (f32[5,4,16]{0,1,2:T(4,128)S(1)}, f32[5,4,16]{0,1,2:T(4,128)S(1)}, u32[]{:S(2)}, u32[]{:S(2)}) collective-permute-start(f32[5,4,16]{0,1,2:T(4,128)S(1)} %bitcast.389), channel_id=1, source_target_pairs={{4,0},{8,4},{12,8},{0,12},{5,1},{9,5},{13,9},{1,13},{6,2},{10,6},{... | collective-permute-start | bytes 3848 | tf_op jit(solution)/shard_map/ppermute | solution.py:17
  7.8 11.2 %collective-permute-start.3 = (f32[5,1,16,128]{3,2,1,0:T(8,128)S(1)}, f32[5,1,16,128]{3,2,1,0:T(8,128)S(1)}, u32[]{:S(2)}, u32[]{:S(2)}) collective-permute-start(f32[5,1,16,128]{3,2,1,0:T(8,128)S(1)} %get-tuple-element.120), channel_id=1, source_target_pairs={{0,1},{1,2},{2,3},{4,5},{5,6},{6,7},{8,9},{9,10},{10,11},{12,13},{... | collective-permute-start | bytes 122888 | tf_op jit(solution)/shard_map/ppermute | solution.py:28
  12.3 6.7 %collective-permute-start.4 = (f32[5,1,16,128]{3,2,1,0:T(8,128)S(1)}, f32[5,1,16,128]{3,2,1,0:T(8,128)S(1)}, u32[]{:S(2)}, u32[]{:S(2)}) collective-permute-start(f32[5,1,16,128]{3,2,1,0:T(8,128)S(1)} %get-tuple-element.121), channel_id=1, source_target_pairs={{1,0},{2,1},{3,2},{5,4},{6,5},{7,6},{9,8},{10,9},{11,10},{13,12},{... | collective-permute-start | bytes 122888 | tf_op jit(solution)/shard_map/ppermute | solution.py:30
  19.5 6.0 %collective-permute-start.1 = (f32[1,5,4,16,128]{4,3,2,1,0:T(8,128)S(1)}, f32[1,5,4,16,128]{4,3,2,1,0:T(8,128)S(1)}, u32[]{:S(2)}, u32[]{:S(2)}) collective-permute-start(f32[1,5,4,16,128]{4,3,2,1,0:T(8,128)S(1)} %collective-permute-done), channel_id=1, source_target_pairs={{0,4},{4,8},{8,12},{12,0},{1,5},{5,9},{9,13},{13,1},{2,6},{6,10},{... | collective-permute-start | bytes 491528 | tf_op jit(solution)/shard_map/ppermute | solution.py:185
  25.5 7.0 %collective-permute-start.2 = (f32[1,5,4,16,128]{4,3,2,1,0:T(8,128)S(1)}, f32[1,5,4,16,128]{4,3,2,1,0:T(8,128)S(1)}, u32[]{:S(2)}, u32[]{:S(2)}) collective-permute-start(f32[1,5,4,16,128]{4,3,2,1,0:T(8,128)S(1)} %collective-permute-done.1), channel_id=1, source_target_pairs={{0,4},{4,8},{8,12},{12,0},{1,5},{5,9},{9,13},{13,1},{2,6},{6,10},{... | collective-permute-start | bytes 491528 | tf_op jit(solution)/shard_map/ppermute | solution.py:185
  34.9 16.8 %collective-permute-start.7 = (f32[1,5,4,16,128]{4,3,2,1,0:T(8,128)S(1)}, f32[1,5,4,16,128]{4,3,2,1,0:T(8,128)S(1)}, u32[]{:S(2)}, u32[]{:S(2)}) collective-permute-start(f32[1,5,4,16,128]{4,3,2,1,0:T(8,128)S(1)} %bitcast.385), channel_id=1, source_target_pairs={{0,4},{4,8},{8,12},{12,0},{1,5},{5,9},{9,13},{13,1},{2,6},{6,10},{... | collective-permute-start | bytes 491528 | tf_op jit(solution)/shard_map/ppermute | solution.py:185
  35.4 12.0 %collective-permute-start.12 = (f32[5,4,16]{0,1,2:T(4,128)S(1)}, f32[5,4,16]{0,1,2:T(4,128)S(1)}, u32[]{:S(2)}, u32[]{:S(2)}) collective-permute-start(f32[5,4,16]{0,1,2:T(4,128)S(1)} %bitcast.392), channel_id=1, source_target_pairs={{12,0},{0,4},{4,8},{8,12},{13,1},{1,5},{5,9},{9,13},{14,2},{2,6},{... | collective-permute-start | bytes 3848 | tf_op jit(solution)/shard_map/ppermute | solution.py:17
  36.0 12.7 %collective-permute-start.13 = (f32[5,4,16]{0,1,2:T(4,128)S(1)}, f32[5,4,16]{0,1,2:T(4,128)S(1)}, u32[]{:S(2)}, u32[]{:S(2)}) collective-permute-start(f32[5,4,16]{0,1,2:T(4,128)S(1)} %bitcast.391), channel_id=1, source_target_pairs={{4,0},{8,4},{12,8},{0,12},{5,1},{9,5},{13,9},{1,13},{6,2},{10,6},{... | collective-permute-start | bytes 3848 | tf_op jit(solution)/shard_map/ppermute | solution.py:17
  39.9 11.2 %collective-permute-start.10 = (f32[5,1,16,128]{3,2,1,0:T(8,128)S(1)}, f32[5,1,16,128]{3,2,1,0:T(8,128)S(1)}, u32[]{:S(2)}, u32[]{:S(2)}) collective-permute-start(f32[5,1,16,128]{3,2,1,0:T(8,128)S(1)} %get-tuple-element.106), channel_id=1, source_target_pairs={{0,1},{1,2},{2,3},{4,5},{5,6},{6,7},{8,9},{9,10},{10,11},{12,13},{... | collective-permute-start | bytes 122888 | tf_op jit(solution)/shard_map/ppermute | solution.py:28
  45.4 5.8 %collective-permute-start.11 = (f32[5,1,16,128]{3,2,1,0:T(8,128)S(1)}, f32[5,1,16,128]{3,2,1,0:T(8,128)S(1)}, u32[]{:S(2)}, u32[]{:S(2)}) collective-permute-start(f32[5,1,16,128]{3,2,1,0:T(8,128)S(1)} %get-tuple-element.107), channel_id=1, source_target_pairs={{1,0},{2,1},{3,2},{5,4},{6,5},{7,6},{9,8},{10,9},{11,10},{13,12},{... | collective-permute-start | bytes 122888 | tf_op jit(solution)/shard_map/ppermute | solution.py:30
  51.7 6.0 %collective-permute-start.8 = (f32[1,5,4,16,128]{4,3,2,1,0:T(8,128)S(1)}, f32[1,5,4,16,128]{4,3,2,1,0:T(8,128)S(1)}, u32[]{:S(2)}, u32[]{:S(2)}) collective-permute-start(f32[1,5,4,16,128]{4,3,2,1,0:T(8,128)S(1)} %collective-permute-done.7), channel_id=1, source_target_pairs={{0,4},{4,8},{8,12},{12,0},{1,5},{5,9},{9,13},{13,1},{2,6},{6,10},{... | collective-permute-start | bytes 491528 | tf_op jit(solution)/shard_map/ppermute | solution.py:185
  57.7 6.7 %collective-permute-start.9 = (f32[1,5,4,16,128]{4,3,2,1,0:T(8,128)S(1)}, f32[1,5,4,16,128]{4,3,2,1,0:T(8,128)S(1)}, u32[]{:S(2)}, u32[]{:S(2)}) collective-permute-start(f32[1,5,4,16,128]{4,3,2,1,0:T(8,128)S(1)} %collective-permute-done.8), channel_id=1, source_target_pairs={{0,4},{4,8},{8,12},{12,0},{1,5},{5,9},{9,13},{13,1},{2,6},{6,10},{... | collective-permute-start | bytes 491528 | tf_op jit(solution)/shard_map/ppermute | solution.py:185
